TPU v7x, 512 devices: a whole 4x8x8 slice. The times are simulated.
512 devices in a mesh: mem: 16 (over y, core), lat: 8 (over x, z_hi), lon: 4 (over z_lo).
Axes of the slice: x: 4, y: 8, z: 8 (z_hi: 2, z_lo: 4; z = z_hi * 4 + z_lo), core: 2. Of those that a mesh axis runs over, the one named last changes fastest.
Arguments:
- members: bfloat16 [32, 8, 256, 512], P('mem', None, 'lat', 'lon'), may hold values from -6 to 6
- increment: float32 [8, 256, 512], P(None, 'lat', 'lon'), may hold values from -6 to 6
Outputs:
- covariance_product: float32 [8, 256, 512], P(None, 'lat', 'lon')
All inputs are finite; a program needn't handle non-finite values.
Results may differ from a plain program's by a relative error of at most 0.0003.
Values sent between devices are 32-bit elements; how exact they have to be, the bound alone decides.
No kernel may reach another device: no remote copies, remote signals or barrier semaphores. Data moves between devices by JAX's collectives and lax.ppermute only.
A program may use at most 64 MiB of HBM per device.

v0:
```python
import jax
import jax.numpy as jnp
from jax import lax
from jax.sharding import PartitionSpec as P

ITERS = 4
factors = (1, 2, 4)
stiffnesses = (1.0, 2.0, 4.0)
weights = (0.5, 0.3, 0.2)


def with_halo(block, sides, width, periodic):
    for axis, dim in sides:
        count = lax.axis_size(axis)
        forward = [(i, i + 1) for i in range(count - 1)]
        if periodic:
            forward.append((count - 1, 0))
        backward = [(target, source) for source, target in forward]
        low = lax.ppermute(
            lax.slice_in_dim(block, block.shape[dim] - width, None, axis=dim), axis, forward
        )
        high = lax.ppermute(lax.slice_in_dim(block, 0, width, axis=dim), axis, backward)
        block = jnp.concatenate([low, block, high], axis=dim)
    return block


def coarsen(values_now, factor):
    if factor == 1:
        return values_now
    dims_now = values_now.shape
    blocks = values_now.reshape(
        dims_now[:-2] + (dims_now[-2] // factor, factor, dims_now[-1] // factor, factor)
    )
    return jnp.mean(blocks, axis=(-3, -1))


def refine(values_now, factor):
    if factor == 1:
        return values_now
    return jnp.repeat(jnp.repeat(values_now, factor, axis=-2), factor, axis=-1)


def diffuse_single(source, stiffness):
    smoothed = source
    for sweeps in range(ITERS):
        with_rows = with_halo(smoothed, (("lat", 2),), 1, False)
        with_cols = with_halo(smoothed, (("lon", 3),), 1, True)
        beside_all = with_rows[:, :, :-2, :] + with_rows[:, :, 2:, :]
        beside_all = beside_all + with_cols[:, :, :, :-2] + with_cols[:, :, :, 2:]
        smoothed = (source + stiffness * beside_all) / (1.0 + 4.0 * stiffness)
    return smoothed


def body(members, increment):
    member_field = members.astype(jnp.float32)
    product = member_field * increment[None]
    running = jnp.zeros(member_field.shape, jnp.float32)
    for factor, stiffness, weight in zip(factors, stiffnesses, weights):
        source = coarsen(product, factor)
        coarse = diffuse_single(source, stiffness)
        running = running + weight * member_field * refine(coarse, factor)
    partial_value = jnp.sum(running, axis=0)
    member_count = members.shape[0] * lax.axis_size("mem")
    summed = lax.psum(partial_value, "mem")
    return summed / (member_count - 1)


def solution(mesh):
    return jax.shard_map(
        body,
        mesh=mesh,
        in_specs=(P("mem", None, "lat", "lon"), P(None, "lat", "lon")),
        out_specs=P(None, "lat", "lon"),
        check_vma=False,
    )
```

profile of v0, /device:TPU:1, one launch (start us, length us, event | category | flops | bytes accessed | tf_op | source)
XLA Modules:
  0.0 434.9 jit_solution(4924736812012016826)
XLA Ops:
  9.0 4.3 copy.364
  13.3 5.6 %reduce_sum.27 = f32[2,8,16,64]{1,3,2,0:T(8,128)S(1)} reduce(f32[2,8,16,2,64,2]{1,5,4,3,2,0:T(2,128)} %bitcast.6, f32[]{:T(128)} %constant.30.clone.1), dimensions={3,5}, to_apply=%region_0.0 | reduce | flops 49152 | bytes 327684 | tf_op jit(solution)/shard_map/reduce_sum | solution.py:34
  20.1 8.4 %collective-permute-start.19 = (f32[2,8,16,1]{3,2,1,0:T(8,128)}, f32[2,8,16,1]{3,2,1,0:T(8,128)}, u32[]{:S(2)}, u32[]{:S(2)}) collective-permute-start(f32[2,8,16,1]{3,2,1,0:T(8,128)} %get-tuple-element.52), channel_id=1, source_target_pairs={{1,0},{2,1},{3,2},{0,3},{5,4},{6,5},{7,6},{4,7},{9,8},{10,9},{11,1... | collective-permute-start | bytes 3080 | tf_op jit(solution)/shard_map/ppermute | solution.py:22
  28.5 3.6 reduce_sum.28
  34.1 3.4 collective-permute-start.34
  38.8 8.6 %collective-permute-start.32 = (f32[2,8,1,32]{1,3,2,0:T(8,128)S(1)}, f32[2,8,1,32]{1,3,2,0:T(8,128)S(1)}, u32[]{:S(2)}, u32[]{:S(2)}) collective-permute-start(f32[2,8,1,32]{1,3,2,0:T(8,128)S(1)} %get-tuple-element.33), channel_id=1, source_target_pairs={{0,4},{4,8},{8,12},{12,16},{16,20},{20,24},{24,28},{1,5},{5,9},{9,... | collective-permute-start | bytes 6152 | tf_op jit(solution)/shard_map/ppermute | solution.py:19
  51.7 4.0 collective-permute-start.39
  58.9 9.4 %collective-permute-start.36 = (f32[2,8,1,32]{1,3,2,0:T(8,128)}, f32[2,8,1,32]{1,3,2,0:T(8,128)}, u32[]{:S(2)}, u32[]{:S(2)}) collective-permute-start(f32[2,8,1,32]{1,3,2,0:T(8,128)} %get-tuple-element.29), channel_id=1, source_target_pairs={{0,4},{4,8},{8,12},{12,16},{16,20},{20,24},{24,28},{1,5},{5,9},{9,... | collective-permute-start | bytes 6152 | tf_op jit(solution)/shard_map/ppermute | solution.py:19
  74.6 8.2 %collective-permute-start.16 = (f32[2,8,1,64]{3,2,1,0:T(1,128)}, f32[2,8,1,64]{3,2,1,0:T(1,128)S(1)}, u32[]{:S(2)}, u32[]{:S(2)}) collective-permute-start(f32[2,8,1,64]{3,2,1,0:T(1,128)} %get-tuple-element.49), channel_id=1, source_target_pairs={{0,4},{4,8},{8,12},{12,16},{16,20},{20,24},{24,28},{1,5},{5,9},{9,... | collective-permute-start | bytes 12296 | tf_op jit(solution)/shard_map/ppermute | solution.py:19
  82.9 5.2 %collective-permute-start.3 = (f32[2,8,32,1]{2,1,3,0:T(8,128)}, f32[2,8,32,1]{2,1,3,0:T(8,128)S(1)}, u32[]{:S(2)}, u32[]{:S(2)}) collective-permute-start(f32[2,8,32,1]{2,1,3,0:T(8,128)} %get-tuple-element.20), channel_id=1, source_target_pairs={{1,0},{2,1},{3,2},{0,3},{5,4},{6,5},{7,6},{4,7},{9,8},{10,9},{11,1... | collective-permute-start | bytes 6152 | tf_op jit(solution)/shard_map/ppermute | solution.py:22
  91.2 3.4 collective-permute-start.43
  97.8 8.8 %collective-permute-start.40 = (f32[2,8,1,32]{1,3,2,0:T(8,128)S(1)}, f32[2,8,1,32]{1,3,2,0:T(8,128)S(1)}, u32[]{:S(2)}, u32[]{:S(2)}) collective-permute-start(f32[2,8,1,32]{1,3,2,0:T(8,128)S(1)} %get-tuple-element.25), channel_id=1, source_target_pairs={{0,4},{4,8},{8,12},{12,16},{16,20},{20,24},{24,28},{1,5},{5,9},{9,... | collective-permute-start | bytes 6152 | tf_op jit(solution)/shard_map/ppermute | solution.py:19
  106.6 5.2 %collective-permute-start.23 = (f32[2,8,16,1]{3,2,1,0:T(8,128)S(1)}, f32[2,8,16,1]{3,2,1,0:T(8,128)S(1)}, u32[]{:S(2)}, u32[]{:S(2)}) collective-permute-start(f32[2,8,16,1]{3,2,1,0:T(8,128)S(1)} %get-tuple-element.48), channel_id=1, source_target_pairs={{1,0},{2,1},{3,2},{0,3},{5,4},{6,5},{7,6},{4,7},{9,8},{10,9},{11,1... | collective-permute-start | bytes 3080 | tf_op jit(solution)/shard_map/ppermute | solution.py:22
  115.1 8.8 %collective-permute-start.20 = (f32[2,8,1,64]{3,2,1,0:T(1,128)S(1)}, f32[2,8,1,64]{3,2,1,0:T(1,128)S(1)}, u32[]{:S(2)}, u32[]{:S(2)}) collective-permute-start(f32[2,8,1,64]{3,2,1,0:T(1,128)S(1)} %get-tuple-element.45), channel_id=1, source_target_pairs={{0,4},{4,8},{8,12},{12,16},{16,20},{20,24},{24,28},{1,5},{5,9},{9,... | collective-permute-start | bytes 12296 | tf_op jit(solution)/shard_map/ppermute | solution.py:19
  128.6 8.8 %collective-permute-start = (f32[2,8,1,128]{3,1,2,0:T(8,128)S(1)}, f32[2,8,1,128]{3,1,2,0:T(8,128)S(1)}, u32[]{:S(2)}, u32[]{:S(2)}) collective-permute-start(f32[2,8,1,128]{3,1,2,0:T(8,128)S(1)} %copy.348), channel_id=1, source_target_pairs={{0,4},{4,8},{8,12},{12,16},{16,20},{20,24},{24,28},{1,5},{5,9},{9,... | collective-permute-start | bytes 24584 | tf_op jit(solution)/shard_map/ppermute | solution.py:19
  137.4 5.2 %collective-permute-start.47 = (f32[2,8,8,1]{1,3,2,0:T(1,128)}, f32[2,8,8,1]{1,3,2,0:T(1,128)}, u32[]{:S(2)}, u32[]{:S(2)}) collective-permute-start(f32[2,8,8,1]{1,3,2,0:T(1,128)} %get-tuple-element.24), channel_id=1, source_target_pairs={{1,0},{2,1},{3,2},{0,3},{5,4},{6,5},{7,6},{4,7},{9,8},{10,9},{11,1... | collective-permute-start | bytes 1544 | tf_op jit(solution)/shard_map/ppermute | solution.py:22
  149.5 8.8 %collective-permute-start.44 = (f32[2,8,1,32]{1,3,2,0:T(8,128)}, f32[2,8,1,32]{1,3,2,0:T(8,128)S(1)}, u32[]{:S(2)}, u32[]{:S(2)}) collective-permute-start(f32[2,8,1,32]{1,3,2,0:T(8,128)} %get-tuple-element.21), channel_id=1, source_target_pairs={{0,4},{4,8},{8,12},{12,16},{16,20},{20,24},{24,28},{1,5},{5,9},{9,... | collective-permute-start | bytes 6152 | tf_op jit(solution)/shard_map/ppermute | solution.py:19
  158.9 5.3 %collective-permute-start.27 = (f32[2,8,16,1]{3,2,1,0:T(8,128)}, f32[2,8,16,1]{3,2,1,0:T(8,128)}, u32[]{:S(2)}, u32[]{:S(2)}) collective-permute-start(f32[2,8,16,1]{3,2,1,0:T(8,128)} %get-tuple-element.44), channel_id=1, source_target_pairs={{1,0},{2,1},{3,2},{0,3},{5,4},{6,5},{7,6},{4,7},{9,8},{10,9},{11,1... | collective-permute-start | bytes 3080 | tf_op jit(solution)/shard_map/ppermute | solution.py:22
  164.2 2.5 fusion.23
  172.8 9.4 %collective-permute-start.24 = (f32[2,8,1,64]{3,2,1,0:T(1,128)}, f32[2,8,1,64]{3,2,1,0:T(1,128)}, u32[]{:S(2)}, u32[]{:S(2)}) collective-permute-start(f32[2,8,1,64]{3,2,1,0:T(1,128)} %get-tuple-element.41), channel_id=1, source_target_pairs={{0,4},{4,8},{8,12},{12,16},{16,20},{20,24},{24,28},{1,5},{5,9},{9,... | collective-permute-start | bytes 12296 | tf_op jit(solution)/shard_map/ppermute | solution.py:19
  187.8 5.1 %collective-permute-start.7 = (f32[2,8,32,1]{2,1,3,0:T(8,128)}, f32[2,8,32,1]{2,1,3,0:T(8,128)S(1)}, u32[]{:S(2)}, u32[]{:S(2)}) collective-permute-start(f32[2,8,32,1]{2,1,3,0:T(8,128)} %get-tuple-element.16), channel_id=1, source_target_pairs={{1,0},{2,1},{3,2},{0,3},{5,4},{6,5},{7,6},{4,7},{9,8},{10,9},{11,1... | collective-permute-start | bytes 6152 | tf_op jit(solution)/shard_map/ppermute | solution.py:22
  199.3 8.2 %collective-permute-start.4 = (f32[2,8,1,128]{3,1,2,0:T(8,128)}, f32[2,8,1,128]{3,1,2,0:T(8,128)S(1)}, u32[]{:S(2)}, u32[]{:S(2)}) collective-permute-start(f32[2,8,1,128]{3,1,2,0:T(8,128)} %copy.352), channel_id=1, source_target_pairs={{0,4},{4,8},{8,12},{12,16},{16,20},{20,24},{24,28},{1,5},{5,9},{9,... | collective-permute-start | bytes 24584 | tf_op jit(solution)/shard_map/ppermute | solution.py:19
  212.4 2.4 fusion.18
  216.8 5.1 %collective-permute-start.11 = (f32[2,8,32,1]{2,1,3,0:T(8,128)}, f32[2,8,32,1]{2,1,3,0:T(8,128)S(1)}, u32[]{:S(2)}, u32[]{:S(2)}) collective-permute-start(f32[2,8,32,1]{2,1,3,0:T(8,128)} %get-tuple-element.12), channel_id=1, source_target_pairs={{1,0},{2,1},{3,2},{0,3},{5,4},{6,5},{7,6},{4,7},{9,8},{10,9},{11,1... | collective-permute-start | bytes 6152 | tf_op jit(solution)/shard_map/ppermute | solution.py:22
  228.3 8.8 %collective-permute-start.8 = (f32[2,8,1,128]{3,1,2,0:T(8,128)}, f32[2,8,1,128]{3,1,2,0:T(8,128)S(1)}, u32[]{:S(2)}, u32[]{:S(2)}) collective-permute-start(f32[2,8,1,128]{3,1,2,0:T(8,128)} %copy.356), channel_id=1, source_target_pairs={{0,4},{4,8},{8,12},{12,16},{16,20},{20,24},{24,28},{1,5},{5,9},{9,... | collective-permute-start | bytes 24584 | tf_op jit(solution)/shard_map/ppermute | solution.py:19
  237.7 5.2 %collective-permute-start.31 = (f32[2,8,16,1]{3,2,1,0:T(8,128)}, f32[2,8,16,1]{3,2,1,0:T(8,128)}, u32[]{:S(2)}, u32[]{:S(2)}) collective-permute-start(f32[2,8,16,1]{3,2,1,0:T(8,128)} %get-tuple-element.40), channel_id=1, source_target_pairs={{1,0},{2,1},{3,2},{0,3},{5,4},{6,5},{7,6},{4,7},{9,8},{10,9},{11,1... | collective-permute-start | bytes 3080 | tf_op jit(solution)/shard_map/ppermute | solution.py:22
  248.9 9.4 %collective-permute-start.28 = (f32[2,8,1,64]{3,2,1,0:T(1,128)}, f32[2,8,1,64]{3,2,1,0:T(1,128)}, u32[]{:S(2)}, u32[]{:S(2)}) collective-permute-start(f32[2,8,1,64]{3,2,1,0:T(1,128)} %get-tuple-element.37), channel_id=1, source_target_pairs={{0,4},{4,8},{8,12},{12,16},{16,20},{20,24},{24,28},{1,5},{5,9},{9,... | collective-permute-start | bytes 12296 | tf_op jit(solution)/shard_map/ppermute | solution.py:19
  258.3 2.4 fusion.13
  262.7 5.1 %collective-permute-start.15 = (f32[2,8,32,1]{2,1,3,0:T(8,128)}, f32[2,8,32,1]{2,1,3,0:T(8,128)S(1)}, u32[]{:S(2)}, u32[]{:S(2)}) collective-permute-start(f32[2,8,32,1]{2,1,3,0:T(8,128)} %get-tuple-element.8), channel_id=1, source_target_pairs={{1,0},{2,1},{3,2},{0,3},{5,4},{6,5},{7,6},{4,7},{9,8},{10,9},{11,1... | collective-permute-start | bytes 6152 | tf_op jit(solution)/shard_map/ppermute | solution.py:22
  274.2 8.8 %collective-permute-start.12 = (f32[2,8,1,128]{3,1,2,0:T(8,128)}, f32[2,8,1,128]{3,1,2,0:T(8,128)}, u32[]{:S(2)}, u32[]{:S(2)}) collective-permute-start(f32[2,8,1,128]{3,1,2,0:T(8,128)} %copy.360), channel_id=1, source_target_pairs={{0,4},{4,8},{8,12},{12,16},{16,20},{20,24},{24,28},{1,5},{5,9},{9,... | collective-permute-start | bytes 24584 | tf_op jit(solution)/shard_map/ppermute | solution.py:19
  289.6 3.2 fusion.3
  294.7 131.7 %all-reduce.2.cloned.1.call-done = f32[8,32,128]{2,1,0:T(8,128)} async-done(((f32[8,32,128]{2,1,0:T(8,128)}), f32[8,32,128]{2,1,0:T(8,128)}) %all-reduce.2.cloned.1.call-update) | async-done | bytes 131088 | tf_op jit(solution)/shard_map/psum | solution.py:64
  (154 shorter events, 98.4 us)
Async XLA Ops:
  6.5 419.9 %all-reduce.2.cloned.1.call-start = ((), (), s32[]{:S(2)}) async-start(), calls=%async_computation | async-start | bytes 262144 | tf_op jit(solution)/shard_map/psum | solution.py:64
  20.1 69.4 %collective-permute-start.19 = (f32[2,8,16,1]{3,2,1,0:T(8,128)}, f32[2,8,16,1]{3,2,1,0:T(8,128)}, u32[]{:S(2)}, u32[]{:S(2)}) collective-permute-start(f32[2,8,16,1]{3,2,1,0:T(8,128)} %get-tuple-element.52), channel_id=1, source_target_pairs={{1,0},{2,1},{3,2},{0,3},{5,4},{6,5},{7,6},{4,7},{9,8},{10,9},{11,1... | collective-permute-start | bytes 3080 | tf_op jit(solution)/shard_map/ppermute | solution.py:22
  32.2 18.0 %collective-permute-start.35 = (f32[2,8,8,1]{1,3,2,0:T(1,128)S(1)}, f32[2,8,8,1]{1,3,2,0:T(1,128)S(1)}, u32[]{:S(2)}, u32[]{:S(2)}) collective-permute-start(f32[2,8,8,1]{1,3,2,0:T(1,128)S(1)} %get-tuple-element.36), channel_id=1, source_target_pairs={{1,0},{2,1},{3,2},{0,3},{5,4},{6,5},{7,6},{4,7},{9,8},{10,9},{11,1... | collective-permute-start | bytes 1544 | tf_op jit(solution)/shard_map/ppermute | solution.py:22
  51.7 19.7 %collective-permute-start.39 = (f32[2,8,8,1]{1,3,2,0:T(1,128)}, f32[2,8,8,1]{1,3,2,0:T(1,128)S(1)}, u32[]{:S(2)}, u32[]{:S(2)}) collective-permute-start(f32[2,8,8,1]{1,3,2,0:T(1,128)} %get-tuple-element.32), channel_id=1, source_target_pairs={{1,0},{2,1},{3,2},{0,3},{5,4},{6,5},{7,6},{4,7},{9,8},{10,9},{11,1... | collective-permute-start | bytes 1544 | tf_op jit(solution)/shard_map/ppermute | solution.py:22
  55.6 17.7 %collective-permute-start.38 = (f32[2,8,8,1]{1,3,2,0:T(1,128)}, f32[2,8,8,1]{1,3,2,0:T(1,128)}, u32[]{:S(2)}, u32[]{:S(2)}) collective-permute-start(f32[2,8,8,1]{1,3,2,0:T(1,128)} %get-tuple-element.31), channel_id=1, source_target_pairs={{0,1},{1,2},{2,3},{3,0},{4,5},{5,6},{6,7},{7,4},{8,9},{9,10},{10,1... | collective-permute-start | bytes 1544 | tf_op jit(solution)/shard_map/ppermute | solution.py:19
  58.9 24.0 %collective-permute-start.36 = (f32[2,8,1,32]{1,3,2,0:T(8,128)}, f32[2,8,1,32]{1,3,2,0:T(8,128)}, u32[]{:S(2)}, u32[]{:S(2)}) collective-permute-start(f32[2,8,1,32]{1,3,2,0:T(8,128)} %get-tuple-element.29), channel_id=1, source_target_pairs={{0,4},{4,8},{8,12},{12,16},{16,20},{20,24},{24,28},{1,5},{5,9},{9,... | collective-permute-start | bytes 6152 | tf_op jit(solution)/shard_map/ppermute | solution.py:19
  71.4 18.1 %collective-permute-start.18 = (f32[2,8,16,1]{3,2,1,0:T(8,128)}, f32[2,8,16,1]{3,2,1,0:T(8,128)S(1)}, u32[]{:S(2)}, u32[]{:S(2)}) collective-permute-start(f32[2,8,16,1]{3,2,1,0:T(8,128)} %get-tuple-element.51), channel_id=1, source_target_pairs={{0,1},{1,2},{2,3},{3,0},{4,5},{5,6},{6,7},{7,4},{8,9},{9,10},{10,1... | collective-permute-start | bytes 3080 | tf_op jit(solution)/shard_map/ppermute | solution.py:19
  82.9 66.6 %collective-permute-start.3 = (f32[2,8,32,1]{2,1,3,0:T(8,128)}, f32[2,8,32,1]{2,1,3,0:T(8,128)S(1)}, u32[]{:S(2)}, u32[]{:S(2)}) collective-permute-start(f32[2,8,32,1]{2,1,3,0:T(8,128)} %get-tuple-element.20), channel_id=1, source_target_pairs={{1,0},{2,1},{3,2},{0,3},{5,4},{6,5},{7,6},{4,7},{9,8},{10,9},{11,1... | collective-permute-start | bytes 6152 | tf_op jit(solution)/shard_map/ppermute | solution.py:22
  96.5 17.2 %collective-permute-start.41 = (f32[2,8,1,32]{1,3,2,0:T(8,128)S(1)}, f32[2,8,1,32]{1,3,2,0:T(8,128)S(1)}, u32[]{:S(2)}, u32[]{:S(2)}) collective-permute-start(f32[2,8,1,32]{1,3,2,0:T(8,128)S(1)} %get-tuple-element.26), channel_id=1, source_target_pairs={{4,0},{8,4},{12,8},{16,12},{20,16},{24,20},{28,24},{5,1},{9,5},{13... | collective-permute-start | bytes 6152 | tf_op jit(solution)/shard_map/ppermute | solution.py:22
  97.8 17.3 %collective-permute-start.40 = (f32[2,8,1,32]{1,3,2,0:T(8,128)S(1)}, f32[2,8,1,32]{1,3,2,0:T(8,128)S(1)}, u32[]{:S(2)}, u32[]{:S(2)}) collective-permute-start(f32[2,8,1,32]{1,3,2,0:T(8,128)S(1)} %get-tuple-element.25), channel_id=1, source_target_pairs={{0,4},{4,8},{8,12},{12,16},{16,20},{20,24},{24,28},{1,5},{5,9},{9,... | collective-permute-start | bytes 6152 | tf_op jit(solution)/shard_map/ppermute | solution.py:19
  106.6 18.7 %collective-permute-start.23 = (f32[2,8,16,1]{3,2,1,0:T(8,128)S(1)}, f32[2,8,16,1]{3,2,1,0:T(8,128)S(1)}, u32[]{:S(2)}, u32[]{:S(2)}) collective-permute-start(f32[2,8,16,1]{3,2,1,0:T(8,128)S(1)} %get-tuple-element.48), channel_id=1, source_target_pairs={{1,0},{2,1},{3,2},{0,3},{5,4},{6,5},{7,6},{4,7},{9,8},{10,9},{11,1... | collective-permute-start | bytes 3080 | tf_op jit(solution)/shard_map/ppermute | solution.py:22
  115.1 22.3 %collective-permute-start.20 = (f32[2,8,1,64]{3,2,1,0:T(1,128)S(1)}, f32[2,8,1,64]{3,2,1,0:T(1,128)S(1)}, u32[]{:S(2)}, u32[]{:S(2)}) collective-permute-start(f32[2,8,1,64]{3,2,1,0:T(1,128)S(1)} %get-tuple-element.45), channel_id=1, source_target_pairs={{0,4},{4,8},{8,12},{12,16},{16,20},{20,24},{24,28},{1,5},{5,9},{9,... | collective-permute-start | bytes 12296 | tf_op jit(solution)/shard_map/ppermute | solution.py:19
  125.3 33.0 %collective-permute-start.2 = (f32[2,8,32,1]{2,1,3,0:T(8,128)}, f32[2,8,32,1]{2,1,3,0:T(8,128)S(1)}, u32[]{:S(2)}, u32[]{:S(2)}) collective-permute-start(f32[2,8,32,1]{2,1,3,0:T(8,128)} %get-tuple-element.19), channel_id=1, source_target_pairs={{0,1},{1,2},{2,3},{3,0},{4,5},{5,6},{6,7},{7,4},{8,9},{9,10},{10,1... | collective-permute-start | bytes 6152 | tf_op jit(solution)/shard_map/ppermute | solution.py:19
  128.6 18.3 %collective-permute-start = (f32[2,8,1,128]{3,1,2,0:T(8,128)S(1)}, f32[2,8,1,128]{3,1,2,0:T(8,128)S(1)}, u32[]{:S(2)}, u32[]{:S(2)}) collective-permute-start(f32[2,8,1,128]{3,1,2,0:T(8,128)S(1)} %copy.348), channel_id=1, source_target_pairs={{0,4},{4,8},{8,12},{12,16},{16,20},{20,24},{24,28},{1,5},{5,9},{9,... | collective-permute-start | bytes 24584 | tf_op jit(solution)/shard_map/ppermute | solution.py:19
  137.4 32.2 %collective-permute-start.47 = (f32[2,8,8,1]{1,3,2,0:T(1,128)}, f32[2,8,8,1]{1,3,2,0:T(1,128)}, u32[]{:S(2)}, u32[]{:S(2)}) collective-permute-start(f32[2,8,8,1]{1,3,2,0:T(1,128)} %get-tuple-element.24), channel_id=1, source_target_pairs={{1,0},{2,1},{3,2},{0,3},{5,4},{6,5},{7,6},{4,7},{9,8},{10,9},{11,1... | collective-permute-start | bytes 1544 | tf_op jit(solution)/shard_map/ppermute | solution.py:22
  143.5 28.0 %collective-permute-start.46 = (f32[2,8,8,1]{1,3,2,0:T(1,128)}, f32[2,8,8,1]{1,3,2,0:T(1,128)}, u32[]{:S(2)}, u32[]{:S(2)}) collective-permute-start(f32[2,8,8,1]{1,3,2,0:T(1,128)} %get-tuple-element.23), channel_id=1, source_target_pairs={{0,1},{1,2},{2,3},{3,0},{4,5},{5,6},{6,7},{7,4},{8,9},{9,10},{10,1... | collective-permute-start | bytes 1544 | tf_op jit(solution)/shard_map/ppermute | solution.py:19
  146.8 26.0 %collective-permute-start.45 = (f32[2,8,1,32]{1,3,2,0:T(8,128)}, f32[2,8,1,32]{1,3,2,0:T(8,128)}, u32[]{:S(2)}, u32[]{:S(2)}) collective-permute-start(f32[2,8,1,32]{1,3,2,0:T(8,128)} %get-tuple-element.22), channel_id=1, source_target_pairs={{4,0},{8,4},{12,8},{16,12},{20,16},{24,20},{28,24},{5,1},{9,5},{13... | collective-permute-start | bytes 6152 | tf_op jit(solution)/shard_map/ppermute | solution.py:22
  149.5 32.7 %collective-permute-start.44 = (f32[2,8,1,32]{1,3,2,0:T(8,128)}, f32[2,8,1,32]{1,3,2,0:T(8,128)S(1)}, u32[]{:S(2)}, u32[]{:S(2)}) collective-permute-start(f32[2,8,1,32]{1,3,2,0:T(8,128)} %get-tuple-element.21), channel_id=1, source_target_pairs={{0,4},{4,8},{8,12},{12,16},{16,20},{20,24},{24,28},{1,5},{5,9},{9,... | collective-permute-start | bytes 6152 | tf_op jit(solution)/shard_map/ppermute | solution.py:19
  158.9 37.2 %collective-permute-start.27 = (f32[2,8,16,1]{3,2,1,0:T(8,128)}, f32[2,8,16,1]{3,2,1,0:T(8,128)}, u32[]{:S(2)}, u32[]{:S(2)}) collective-permute-start(f32[2,8,16,1]{3,2,1,0:T(8,128)} %get-tuple-element.44), channel_id=1, source_target_pairs={{1,0},{2,1},{3,2},{0,3},{5,4},{6,5},{7,6},{4,7},{9,8},{10,9},{11,1... | collective-permute-start | bytes 3080 | tf_op jit(solution)/shard_map/ppermute | solution.py:22
  169.6 28.4 %collective-permute-start.26 = (f32[2,8,16,1]{3,2,1,0:T(8,128)}, f32[2,8,16,1]{3,2,1,0:T(8,128)}, u32[]{:S(2)}, u32[]{:S(2)}) collective-permute-start(f32[2,8,16,1]{3,2,1,0:T(8,128)} %get-tuple-element.43), channel_id=1, source_target_pairs={{0,1},{1,2},{2,3},{3,0},{4,5},{5,6},{6,7},{7,4},{8,9},{9,10},{10,1... | collective-permute-start | bytes 3080 | tf_op jit(solution)/shard_map/ppermute | solution.py:19
  171.5 27.8 %collective-permute-start.25 = (f32[2,8,1,64]{3,2,1,0:T(1,128)}, f32[2,8,1,64]{3,2,1,0:T(1,128)S(1)}, u32[]{:S(2)}, u32[]{:S(2)}) collective-permute-start(f32[2,8,1,64]{3,2,1,0:T(1,128)} %get-tuple-element.42), channel_id=1, source_target_pairs={{4,0},{8,4},{12,8},{16,12},{20,16},{24,20},{28,24},{5,1},{9,5},{13... | collective-permute-start | bytes 12296 | tf_op jit(solution)/shard_map/ppermute | solution.py:22
  172.8 34.8 %collective-permute-start.24 = (f32[2,8,1,64]{3,2,1,0:T(1,128)}, f32[2,8,1,64]{3,2,1,0:T(1,128)}, u32[]{:S(2)}, u32[]{:S(2)}) collective-permute-start(f32[2,8,1,64]{3,2,1,0:T(1,128)} %get-tuple-element.41), channel_id=1, source_target_pairs={{0,4},{4,8},{8,12},{12,16},{16,20},{20,24},{24,28},{1,5},{5,9},{9,... | collective-permute-start | bytes 12296 | tf_op jit(solution)/shard_map/ppermute | solution.py:19
  187.8 24.6 %collective-permute-start.7 = (f32[2,8,32,1]{2,1,3,0:T(8,128)}, f32[2,8,32,1]{2,1,3,0:T(8,128)S(1)}, u32[]{:S(2)}, u32[]{:S(2)}) collective-permute-start(f32[2,8,32,1]{2,1,3,0:T(8,128)} %get-tuple-element.16), channel_id=1, source_target_pairs={{1,0},{2,1},{3,2},{0,3},{5,4},{6,5},{7,6},{4,7},{9,8},{10,9},{11,1... | collective-permute-start | bytes 6152 | tf_op jit(solution)/shard_map/ppermute | solution.py:22
  216.8 32.0 %collective-permute-start.11 = (f32[2,8,32,1]{2,1,3,0:T(8,128)}, f32[2,8,32,1]{2,1,3,0:T(8,128)S(1)}, u32[]{:S(2)}, u32[]{:S(2)}) collective-permute-start(f32[2,8,32,1]{2,1,3,0:T(8,128)} %get-tuple-element.12), channel_id=1, source_target_pairs={{1,0},{2,1},{3,2},{0,3},{5,4},{6,5},{7,6},{4,7},{9,8},{10,9},{11,1... | collective-permute-start | bytes 6152 | tf_op jit(solution)/shard_map/ppermute | solution.py:22
  222.0 36.3 %collective-permute-start.10 = (f32[2,8,32,1]{2,1,3,0:T(8,128)}, f32[2,8,32,1]{2,1,3,0:T(8,128)}, u32[]{:S(2)}, u32[]{:S(2)}) collective-permute-start(f32[2,8,32,1]{2,1,3,0:T(8,128)} %get-tuple-element.11), channel_id=1, source_target_pairs={{0,1},{1,2},{2,3},{3,0},{4,5},{5,6},{6,7},{7,4},{8,9},{9,10},{10,1... | collective-permute-start | bytes 6152 | tf_op jit(solution)/shard_map/ppermute | solution.py:19
  228.3 17.9 %collective-permute-start.8 = (f32[2,8,1,128]{3,1,2,0:T(8,128)}, f32[2,8,1,128]{3,1,2,0:T(8,128)S(1)}, u32[]{:S(2)}, u32[]{:S(2)}) collective-permute-start(f32[2,8,1,128]{3,1,2,0:T(8,128)} %copy.356), channel_id=1, source_target_pairs={{0,4},{4,8},{8,12},{12,16},{16,20},{20,24},{24,28},{1,5},{5,9},{9,... | collective-permute-start | bytes 24584 | tf_op jit(solution)/shard_map/ppermute | solution.py:19
  237.7 33.2 %collective-permute-start.31 = (f32[2,8,16,1]{3,2,1,0:T(8,128)}, f32[2,8,16,1]{3,2,1,0:T(8,128)}, u32[]{:S(2)}, u32[]{:S(2)}) collective-permute-start(f32[2,8,16,1]{3,2,1,0:T(8,128)} %get-tuple-element.40), channel_id=1, source_target_pairs={{1,0},{2,1},{3,2},{0,3},{5,4},{6,5},{7,6},{4,7},{9,8},{10,9},{11,1... | collective-permute-start | bytes 3080 | tf_op jit(solution)/shard_map/ppermute | solution.py:22
  242.9 30.0 %collective-permute-start.30 = (f32[2,8,16,1]{3,2,1,0:T(8,128)S(1)}, f32[2,8,16,1]{3,2,1,0:T(8,128)}, u32[]{:S(2)}, u32[]{:S(2)}) collective-permute-start(f32[2,8,16,1]{3,2,1,0:T(8,128)S(1)} %get-tuple-element.39), channel_id=1, source_target_pairs={{0,1},{1,2},{2,3},{3,0},{4,5},{5,6},{6,7},{7,4},{8,9},{9,10},{10,1... | collective-permute-start | bytes 3080 | tf_op jit(solution)/shard_map/ppermute | solution.py:19
  246.2 27.9 %collective-permute-start.29 = (f32[2,8,1,64]{3,2,1,0:T(1,128)}, f32[2,8,1,64]{3,2,1,0:T(1,128)S(1)}, u32[]{:S(2)}, u32[]{:S(2)}) collective-permute-start(f32[2,8,1,64]{3,2,1,0:T(1,128)} %get-tuple-element.38), channel_id=1, source_target_pairs={{4,0},{8,4},{12,8},{16,12},{20,16},{24,20},{28,24},{5,1},{9,5},{13... | collective-permute-start | bytes 12296 | tf_op jit(solution)/shard_map/ppermute | solution.py:22
  248.9 34.1 %collective-permute-start.28 = (f32[2,8,1,64]{3,2,1,0:T(1,128)}, f32[2,8,1,64]{3,2,1,0:T(1,128)}, u32[]{:S(2)}, u32[]{:S(2)}) collective-permute-start(f32[2,8,1,64]{3,2,1,0:T(1,128)} %get-tuple-element.37), channel_id=1, source_target_pairs={{0,4},{4,8},{8,12},{12,16},{16,20},{20,24},{24,28},{1,5},{5,9},{9,... | collective-permute-start | bytes 12296 | tf_op jit(solution)/shard_map/ppermute | solution.py:19
  262.7 25.8 %collective-permute-start.15 = (f32[2,8,32,1]{2,1,3,0:T(8,128)}, f32[2,8,32,1]{2,1,3,0:T(8,128)S(1)}, u32[]{:S(2)}, u32[]{:S(2)}) collective-permute-start(f32[2,8,32,1]{2,1,3,0:T(8,128)} %get-tuple-element.8), channel_id=1, source_target_pairs={{1,0},{2,1},{3,2},{0,3},{5,4},{6,5},{7,6},{4,7},{9,8},{10,9},{11,1... | collective-permute-start | bytes 6152 | tf_op jit(solution)/shard_map/ppermute | solution.py:22
  270.9 17.5 %collective-permute-start.14 = (f32[2,8,32,1]{2,1,3,0:T(8,128)}, f32[2,8,32,1]{2,1,3,0:T(8,128)}, u32[]{:S(2)}, u32[]{:S(2)}) collective-permute-start(f32[2,8,32,1]{2,1,3,0:T(8,128)} %get-tuple-element.7), channel_id=1, source_target_pairs={{0,1},{1,2},{2,3},{3,0},{4,5},{5,6},{6,7},{7,4},{8,9},{9,10},{10,1... | collective-permute-start | bytes 6152 | tf_op jit(solution)/shard_map/ppermute | solution.py:19
  (25 other events, 343.9 us)
Sparse Core Ops, SparseCore 0:
  294.8 131.5 all-reduce.1
where the time goes:
time: 437 us; the launch traced here: 435 us
  starting transfers between devices  205 us (47%)
  waiting for transfers between devices  132 us (30%)
  local copies, waits for them, and re-layouts  54.8 us (13%)
  other arithmetic  29 us (7%)
  between operations  14.2 us (3%)
    psum x1, waiting for transfers between devices, body(): summed = lax.psum(partial_value, 'mem')  132 us
    ppermute x24, starting transfers between devices, with_halo(): lax.ppermute(lax.slice_in_dim(block, block.shape[dim] - width, None, axis...  130 us
    ppermute x24, starting transfers between devices, with_halo(): lax.ppermute(lax.slice_in_dim(block, 0, width, axis=dim), axis, backward)  74.5 us
    slice x28, local copies, waits for them, and re-layouts, with_halo(): lax.slice_in_dim(block, block.shape[dim] - width, None, axis=dim)  19.6 us
    div x11, other arithmetic, diffuse_single(): smoothed = (source + stiffness * beside_all) / (1.0 + 4.0 * stiffness)  14.9 us
    reduce_sum x2, other arithmetic, coarsen(): return jnp.mean(blocks, axis=(-3, -1))  9.21 us
  transfers between devices with their start and end apart: 49, of which 1 were waited for; matrix products, arithmetic and copies ran while one was open for 13% of the time, Pallas kernels for 0%

commit v1 on v0

--- a/solution.py
+++ b/solution.py
@@ -61,7 +61,7 @@
         running = running + weight * member_field * refine(coarse, factor)
     partial_value = jnp.sum(running, axis=0)
     member_count = members.shape[0] * lax.axis_size("mem")
-    summed = lax.psum(partial_value, "mem")
+    summed = jnp.sum(lax.all_gather(partial_value, "mem"), axis=0)
     return summed / (member_count - 1)
 
 

time: 437 us -> 365 us (0.84)
  waiting for transfers between devices: 132 us -> 59.3 us
    psum x1 -> x0, waiting for transfers between devices: 132 us -> none  [body(): summed = lax.psum(partial_value, 'mem')]
    all_gather x0 -> x1, waiting for transfers between devices: none -> 59.1 us  [body(): summed = jnp.sum(lax.all_gather(partial_value, 'mem'), axis=0)]
  transfers between devices with their start and end apart: 49 -> 49, of which waited for: 1 -> 1; matrix products, arithmetic and copies ran while one was open for 13% -> 16% of each run, Pallas kernels for 0% -> 0%
where the time goes in v1:
time: 365 us; the launch traced here: 363 us
  starting transfers between devices  205 us (56%)
  waiting for transfers between devices  59.3 us (16%)
  local copies, waits for them, and re-layouts  54.8 us (15%)
  other arithmetic  29.9 us (8%)
  between operations  14.2 us (4%)
    ppermute x24, starting transfers between devices, with_halo(): lax.ppermute(lax.slice_in_dim(block, block.shape[dim] - width, None, axis...  130 us
    ppermute x24, starting transfers between devices, with_halo(): lax.ppermute(lax.slice_in_dim(block, 0, width, axis=dim), axis, backward)  74.5 us
    all_gather x1, waiting for transfers between devices, body(): summed = jnp.sum(lax.all_gather(partial_value, 'mem'), axis=0)  59.1 us
    slice x28, local copies, waits for them, and re-layouts, with_halo(): lax.slice_in_dim(block, block.shape[dim] - width, None, axis=dim)  19.6 us
    div x11, other arithmetic, diffuse_single(): smoothed = (source + stiffness * beside_all) / (1.0 + 4.0 * stiffness)  14.9 us
    reduce_sum x2, other arithmetic, coarsen(): return jnp.mean(blocks, axis=(-3, -1))  9.21 us
    slice x4, local copies, waits for them, and re-layouts, with_halo(): lax.slice_in_dim(block, 0, width, axis=dim)  8.59 us
  transfers between devices with their start and end apart: 49, of which 1 were waited for; matrix products, arithmetic and copies ran while one was open for 16% of the time, Pallas kernels for 0%

profile of v1, /device:TPU:1, one launch (start us, length us, event | category | flops | bytes accessed | tf_op | source)
XLA Modules:
  0.0 363.1 jit_solution(1750462996131178324)
XLA Ops:
  9.0 4.3 %copy.364 = f32[2,8,32,128]{1,3,2,0:T(8,128)} copy(f32[2,8,32,128]{2,1,3,0:T(8,128)S(1)} %convert_multiply_fusion.2) | data formatting | bytes 524288 | tf_op jit(solution)/shard_map/mul | solution.py:56
  13.3 5.6 %reduce_sum.36 = f32[2,8,16,64]{1,3,2,0:T(8,128)S(1)} reduce(f32[2,8,16,2,64,2]{1,5,4,3,2,0:T(2,128)} %bitcast.7, f32[]{:T(128)} %constant.30.clone.1), dimensions={3,5}, to_apply=%region_0.0 | reduce | flops 49152 | bytes 327684 | tf_op jit(solution)/shard_map/reduce_sum | solution.py:34
  20.1 8.4 %collective-permute-start.19 = (f32[2,8,16,1]{3,2,1,0:T(8,128)}, f32[2,8,16,1]{3,2,1,0:T(8,128)}, u32[]{:S(2)}, u32[]{:S(2)}) collective-permute-start(f32[2,8,16,1]{3,2,1,0:T(8,128)} %get-tuple-element.52), channel_id=1, source_target_pairs={{1,0},{2,1},{3,2},{0,3},{5,4},{6,5},{7,6},{4,7},{9,8},{10,9},{11,1... | collective-permute-start | bytes 3080 | tf_op jit(solution)/shard_map/ppermute | solution.py:22
  28.5 3.6 reduce_sum.37
  34.1 3.4 collective-permute-start.34
  38.8 8.6 %collective-permute-start.32 = (f32[2,8,1,32]{1,3,2,0:T(8,128)S(1)}, f32[2,8,1,32]{1,3,2,0:T(8,128)S(1)}, u32[]{:S(2)}, u32[]{:S(2)}) collective-permute-start(f32[2,8,1,32]{1,3,2,0:T(8,128)S(1)} %get-tuple-element.33), channel_id=1, source_target_pairs={{0,4},{4,8},{8,12},{12,16},{16,20},{20,24},{24,28},{1,5},{5,9},{9,... | collective-permute-start | bytes 6152 | tf_op jit(solution)/shard_map/ppermute | solution.py:19
  51.7 4.0 %collective-permute-start.39 = (f32[2,8,8,1]{1,3,2,0:T(1,128)}, f32[2,8,8,1]{1,3,2,0:T(1,128)S(1)}, u32[]{:S(2)}, u32[]{:S(2)}) collective-permute-start(f32[2,8,8,1]{1,3,2,0:T(1,128)} %get-tuple-element.32), channel_id=1, source_target_pairs={{1,0},{2,1},{3,2},{0,3},{5,4},{6,5},{7,6},{4,7},{9,8},{10,9},{11,1... | collective-permute-start | bytes 1544 | tf_op jit(solution)/shard_map/ppermute | solution.py:22
  58.9 9.4 %collective-permute-start.36 = (f32[2,8,1,32]{1,3,2,0:T(8,128)}, f32[2,8,1,32]{1,3,2,0:T(8,128)}, u32[]{:S(2)}, u32[]{:S(2)}) collective-permute-start(f32[2,8,1,32]{1,3,2,0:T(8,128)} %get-tuple-element.29), channel_id=1, source_target_pairs={{0,4},{4,8},{8,12},{12,16},{16,20},{20,24},{24,28},{1,5},{5,9},{9,... | collective-permute-start | bytes 6152 | tf_op jit(solution)/shard_map/ppermute | solution.py:19
  74.6 8.2 %collective-permute-start.16 = (f32[2,8,1,64]{3,2,1,0:T(1,128)}, f32[2,8,1,64]{3,2,1,0:T(1,128)S(1)}, u32[]{:S(2)}, u32[]{:S(2)}) collective-permute-start(f32[2,8,1,64]{3,2,1,0:T(1,128)} %get-tuple-element.49), channel_id=1, source_target_pairs={{0,4},{4,8},{8,12},{12,16},{16,20},{20,24},{24,28},{1,5},{5,9},{9,... | collective-permute-start | bytes 12296 | tf_op jit(solution)/shard_map/ppermute | solution.py:19
  82.9 5.2 %collective-permute-start.3 = (f32[2,8,32,1]{2,1,3,0:T(8,128)}, f32[2,8,32,1]{2,1,3,0:T(8,128)S(1)}, u32[]{:S(2)}, u32[]{:S(2)}) collective-permute-start(f32[2,8,32,1]{2,1,3,0:T(8,128)} %get-tuple-element.20), channel_id=1, source_target_pairs={{1,0},{2,1},{3,2},{0,3},{5,4},{6,5},{7,6},{4,7},{9,8},{10,9},{11,1... | collective-permute-start | bytes 6152 | tf_op jit(solution)/shard_map/ppermute | solution.py:22
  91.2 3.4 collective-permute-start.43
  97.8 8.8 %collective-permute-start.40 = (f32[2,8,1,32]{1,3,2,0:T(8,128)S(1)}, f32[2,8,1,32]{1,3,2,0:T(8,128)S(1)}, u32[]{:S(2)}, u32[]{:S(2)}) collective-permute-start(f32[2,8,1,32]{1,3,2,0:T(8,128)S(1)} %get-tuple-element.25), channel_id=1, source_target_pairs={{0,4},{4,8},{8,12},{12,16},{16,20},{20,24},{24,28},{1,5},{5,9},{9,... | collective-permute-start | bytes 6152 | tf_op jit(solution)/shard_map/ppermute | solution.py:19
  106.6 5.2 %collective-permute-start.23 = (f32[2,8,16,1]{3,2,1,0:T(8,128)S(1)}, f32[2,8,16,1]{3,2,1,0:T(8,128)S(1)}, u32[]{:S(2)}, u32[]{:S(2)}) collective-permute-start(f32[2,8,16,1]{3,2,1,0:T(8,128)S(1)} %get-tuple-element.48), channel_id=1, source_target_pairs={{1,0},{2,1},{3,2},{0,3},{5,4},{6,5},{7,6},{4,7},{9,8},{10,9},{11,1... | collective-permute-start | bytes 3080 | tf_op jit(solution)/shard_map/ppermute | solution.py:22
  115.1 8.8 %collective-permute-start.20 = (f32[2,8,1,64]{3,2,1,0:T(1,128)S(1)}, f32[2,8,1,64]{3,2,1,0:T(1,128)S(1)}, u32[]{:S(2)}, u32[]{:S(2)}) collective-permute-start(f32[2,8,1,64]{3,2,1,0:T(1,128)S(1)} %get-tuple-element.45), channel_id=1, source_target_pairs={{0,4},{4,8},{8,12},{12,16},{16,20},{20,24},{24,28},{1,5},{5,9},{9,... | collective-permute-start | bytes 12296 | tf_op jit(solution)/shard_map/ppermute | solution.py:19
  128.6 8.8 %collective-permute-start = (f32[2,8,1,128]{3,1,2,0:T(8,128)S(1)}, f32[2,8,1,128]{3,1,2,0:T(8,128)S(1)}, u32[]{:S(2)}, u32[]{:S(2)}) collective-permute-start(f32[2,8,1,128]{3,1,2,0:T(8,128)S(1)} %copy.348), channel_id=1, source_target_pairs={{0,4},{4,8},{8,12},{12,16},{16,20},{20,24},{24,28},{1,5},{5,9},{9,... | collective-permute-start | bytes 24584 | tf_op jit(solution)/shard_map/ppermute | solution.py:19
  137.4 5.2 %collective-permute-start.47 = (f32[2,8,8,1]{1,3,2,0:T(1,128)}, f32[2,8,8,1]{1,3,2,0:T(1,128)}, u32[]{:S(2)}, u32[]{:S(2)}) collective-permute-start(f32[2,8,8,1]{1,3,2,0:T(1,128)} %get-tuple-element.24), channel_id=1, source_target_pairs={{1,0},{2,1},{3,2},{0,3},{5,4},{6,5},{7,6},{4,7},{9,8},{10,9},{11,1... | collective-permute-start | bytes 1544 | tf_op jit(solution)/shard_map/ppermute | solution.py:22
  149.5 8.8 %collective-permute-start.44 = (f32[2,8,1,32]{1,3,2,0:T(8,128)}, f32[2,8,1,32]{1,3,2,0:T(8,128)S(1)}, u32[]{:S(2)}, u32[]{:S(2)}) collective-permute-start(f32[2,8,1,32]{1,3,2,0:T(8,128)} %get-tuple-element.21), channel_id=1, source_target_pairs={{0,4},{4,8},{8,12},{12,16},{16,20},{20,24},{24,28},{1,5},{5,9},{9,... | collective-permute-start | bytes 6152 | tf_op jit(solution)/shard_map/ppermute | solution.py:19
  158.9 5.3 %collective-permute-start.27 = (f32[2,8,16,1]{3,2,1,0:T(8,128)}, f32[2,8,16,1]{3,2,1,0:T(8,128)}, u32[]{:S(2)}, u32[]{:S(2)}) collective-permute-start(f32[2,8,16,1]{3,2,1,0:T(8,128)} %get-tuple-element.44), channel_id=1, source_target_pairs={{1,0},{2,1},{3,2},{0,3},{5,4},{6,5},{7,6},{4,7},{9,8},{10,9},{11,1... | collective-permute-start | bytes 3080 | tf_op jit(solution)/shard_map/ppermute | solution.py:22
  164.2 2.5 fusion.23
  172.8 9.4 %collective-permute-start.24 = (f32[2,8,1,64]{3,2,1,0:T(1,128)}, f32[2,8,1,64]{3,2,1,0:T(1,128)}, u32[]{:S(2)}, u32[]{:S(2)}) collective-permute-start(f32[2,8,1,64]{3,2,1,0:T(1,128)} %get-tuple-element.41), channel_id=1, source_target_pairs={{0,4},{4,8},{8,12},{12,16},{16,20},{20,24},{24,28},{1,5},{5,9},{9,... | collective-permute-start | bytes 12296 | tf_op jit(solution)/shard_map/ppermute | solution.py:19
  187.8 5.1 %collective-permute-start.7 = (f32[2,8,32,1]{2,1,3,0:T(8,128)}, f32[2,8,32,1]{2,1,3,0:T(8,128)S(1)}, u32[]{:S(2)}, u32[]{:S(2)}) collective-permute-start(f32[2,8,32,1]{2,1,3,0:T(8,128)} %get-tuple-element.16), channel_id=1, source_target_pairs={{1,0},{2,1},{3,2},{0,3},{5,4},{6,5},{7,6},{4,7},{9,8},{10,9},{11,1... | collective-permute-start | bytes 6152 | tf_op jit(solution)/shard_map/ppermute | solution.py:22
  199.3 8.2 %collective-permute-start.4 = (f32[2,8,1,128]{3,1,2,0:T(8,128)}, f32[2,8,1,128]{3,1,2,0:T(8,128)S(1)}, u32[]{:S(2)}, u32[]{:S(2)}) collective-permute-start(f32[2,8,1,128]{3,1,2,0:T(8,128)} %copy.352), channel_id=1, source_target_pairs={{0,4},{4,8},{8,12},{12,16},{16,20},{20,24},{24,28},{1,5},{5,9},{9,... | collective-permute-start | bytes 24584 | tf_op jit(solution)/shard_map/ppermute | solution.py:19
  212.4 2.4 fusion.18
  216.8 5.1 %collective-permute-start.11 = (f32[2,8,32,1]{2,1,3,0:T(8,128)}, f32[2,8,32,1]{2,1,3,0:T(8,128)S(1)}, u32[]{:S(2)}, u32[]{:S(2)}) collective-permute-start(f32[2,8,32,1]{2,1,3,0:T(8,128)} %get-tuple-element.12), channel_id=1, source_target_pairs={{1,0},{2,1},{3,2},{0,3},{5,4},{6,5},{7,6},{4,7},{9,8},{10,9},{11,1... | collective-permute-start | bytes 6152 | tf_op jit(solution)/shard_map/ppermute | solution.py:22
  228.3 8.8 %collective-permute-start.8 = (f32[2,8,1,128]{3,1,2,0:T(8,128)}, f32[2,8,1,128]{3,1,2,0:T(8,128)S(1)}, u32[]{:S(2)}, u32[]{:S(2)}) collective-permute-start(f32[2,8,1,128]{3,1,2,0:T(8,128)} %copy.356), channel_id=1, source_target_pairs={{0,4},{4,8},{8,12},{12,16},{16,20},{20,24},{24,28},{1,5},{5,9},{9,... | collective-permute-start | bytes 24584 | tf_op jit(solution)/shard_map/ppermute | solution.py:19
  237.7 5.2 %collective-permute-start.31 = (f32[2,8,16,1]{3,2,1,0:T(8,128)}, f32[2,8,16,1]{3,2,1,0:T(8,128)}, u32[]{:S(2)}, u32[]{:S(2)}) collective-permute-start(f32[2,8,16,1]{3,2,1,0:T(8,128)} %get-tuple-element.40), channel_id=1, source_target_pairs={{1,0},{2,1},{3,2},{0,3},{5,4},{6,5},{7,6},{4,7},{9,8},{10,9},{11,1... | collective-permute-start | bytes 3080 | tf_op jit(solution)/shard_map/ppermute | solution.py:22
  248.9 9.4 %collective-permute-start.28 = (f32[2,8,1,64]{3,2,1,0:T(1,128)}, f32[2,8,1,64]{3,2,1,0:T(1,128)}, u32[]{:S(2)}, u32[]{:S(2)}) collective-permute-start(f32[2,8,1,64]{3,2,1,0:T(1,128)} %get-tuple-element.37), channel_id=1, source_target_pairs={{0,4},{4,8},{8,12},{12,16},{16,20},{20,24},{24,28},{1,5},{5,9},{9,... | collective-permute-start | bytes 12296 | tf_op jit(solution)/shard_map/ppermute | solution.py:19
  258.3 2.4 fusion.13
  262.7 5.1 %collective-permute-start.15 = (f32[2,8,32,1]{2,1,3,0:T(8,128)}, f32[2,8,32,1]{2,1,3,0:T(8,128)S(1)}, u32[]{:S(2)}, u32[]{:S(2)}) collective-permute-start(f32[2,8,32,1]{2,1,3,0:T(8,128)} %get-tuple-element.8), channel_id=1, source_target_pairs={{1,0},{2,1},{3,2},{0,3},{5,4},{6,5},{7,6},{4,7},{9,8},{10,9},{11,1... | collective-permute-start | bytes 6152 | tf_op jit(solution)/shard_map/ppermute | solution.py:22
  274.2 8.8 %collective-permute-start.12 = (f32[2,8,1,128]{3,1,2,0:T(8,128)}, f32[2,8,1,128]{3,1,2,0:T(8,128)}, u32[]{:S(2)}, u32[]{:S(2)}) collective-permute-start(f32[2,8,1,128]{3,1,2,0:T(8,128)} %copy.360), channel_id=1, source_target_pairs={{0,4},{4,8},{8,12},{12,16},{16,20},{20,24},{24,28},{1,5},{5,9},{9,... | collective-permute-start | bytes 24584 | tf_op jit(solution)/shard_map/ppermute | solution.py:19
  289.6 3.2 fusion.3
  294.7 59.1 %all-gather.3.cloned.1.call-done = f32[128,32,128]{2,1,0:T(8,128)} async-done(((f32[8,32,128]{2,1,0:T(8,128)}), f32[128,32,128]{2,1,0:T(8,128)}) %all-gather.3.cloned.1.call-update) | async-done | bytes 2097168 | tf_op jit(solution)/shard_map/all_gather | solution.py:64
  (155 shorter events, 99.2 us)
Async XLA Ops:
  6.5 347.3 %all-gather.3.cloned.1.call-start = ((), (), s32[]{:S(2)}) async-start(), calls=%async_computation | async-start | bytes 2228224 | tf_op jit(solution)/shard_map/all_gather | solution.py:64
  20.1 69.4 %collective-permute-start.19 = (f32[2,8,16,1]{3,2,1,0:T(8,128)}, f32[2,8,16,1]{3,2,1,0:T(8,128)}, u32[]{:S(2)}, u32[]{:S(2)}) collective-permute-start(f32[2,8,16,1]{3,2,1,0:T(8,128)} %get-tuple-element.52), channel_id=1, source_target_pairs={{1,0},{2,1},{3,2},{0,3},{5,4},{6,5},{7,6},{4,7},{9,8},{10,9},{11,1... | collective-permute-start | bytes 3080 | tf_op jit(solution)/shard_map/ppermute | solution.py:22
  32.2 18.0 %collective-permute-start.35 = (f32[2,8,8,1]{1,3,2,0:T(1,128)S(1)}, f32[2,8,8,1]{1,3,2,0:T(1,128)S(1)}, u32[]{:S(2)}, u32[]{:S(2)}) collective-permute-start(f32[2,8,8,1]{1,3,2,0:T(1,128)S(1)} %get-tuple-element.36), channel_id=1, source_target_pairs={{1,0},{2,1},{3,2},{0,3},{5,4},{6,5},{7,6},{4,7},{9,8},{10,9},{11,1... | collective-permute-start | bytes 1544 | tf_op jit(solution)/shard_map/ppermute | solution.py:22
  51.7 19.7 %collective-permute-start.39 = (f32[2,8,8,1]{1,3,2,0:T(1,128)}, f32[2,8,8,1]{1,3,2,0:T(1,128)S(1)}, u32[]{:S(2)}, u32[]{:S(2)}) collective-permute-start(f32[2,8,8,1]{1,3,2,0:T(1,128)} %get-tuple-element.32), channel_id=1, source_target_pairs={{1,0},{2,1},{3,2},{0,3},{5,4},{6,5},{7,6},{4,7},{9,8},{10,9},{11,1... | collective-permute-start | bytes 1544 | tf_op jit(solution)/shard_map/ppermute | solution.py:22
  55.6 17.7 %collective-permute-start.38 = (f32[2,8,8,1]{1,3,2,0:T(1,128)}, f32[2,8,8,1]{1,3,2,0:T(1,128)}, u32[]{:S(2)}, u32[]{:S(2)}) collective-permute-start(f32[2,8,8,1]{1,3,2,0:T(1,128)} %get-tuple-element.31), channel_id=1, source_target_pairs={{0,1},{1,2},{2,3},{3,0},{4,5},{5,6},{6,7},{7,4},{8,9},{9,10},{10,1... | collective-permute-start | bytes 1544 | tf_op jit(solution)/shard_map/ppermute | solution.py:19
  58.9 24.0 %collective-permute-start.36 = (f32[2,8,1,32]{1,3,2,0:T(8,128)}, f32[2,8,1,32]{1,3,2,0:T(8,128)}, u32[]{:S(2)}, u32[]{:S(2)}) collective-permute-start(f32[2,8,1,32]{1,3,2,0:T(8,128)} %get-tuple-element.29), channel_id=1, source_target_pairs={{0,4},{4,8},{8,12},{12,16},{16,20},{20,24},{24,28},{1,5},{5,9},{9,... | collective-permute-start | bytes 6152 | tf_op jit(solution)/shard_map/ppermute | solution.py:19
  71.4 18.1 %collective-permute-start.18 = (f32[2,8,16,1]{3,2,1,0:T(8,128)}, f32[2,8,16,1]{3,2,1,0:T(8,128)S(1)}, u32[]{:S(2)}, u32[]{:S(2)}) collective-permute-start(f32[2,8,16,1]{3,2,1,0:T(8,128)} %get-tuple-element.51), channel_id=1, source_target_pairs={{0,1},{1,2},{2,3},{3,0},{4,5},{5,6},{6,7},{7,4},{8,9},{9,10},{10,1... | collective-permute-start | bytes 3080 | tf_op jit(solution)/shard_map/ppermute | solution.py:19
  82.9 66.6 %collective-permute-start.3 = (f32[2,8,32,1]{2,1,3,0:T(8,128)}, f32[2,8,32,1]{2,1,3,0:T(8,128)S(1)}, u32[]{:S(2)}, u32[]{:S(2)}) collective-permute-start(f32[2,8,32,1]{2,1,3,0:T(8,128)} %get-tuple-element.20), channel_id=1, source_target_pairs={{1,0},{2,1},{3,2},{0,3},{5,4},{6,5},{7,6},{4,7},{9,8},{10,9},{11,1... | collective-permute-start | bytes 6152 | tf_op jit(solution)/shard_map/ppermute | solution.py:22
  96.5 17.2 %collective-permute-start.41 = (f32[2,8,1,32]{1,3,2,0:T(8,128)S(1)}, f32[2,8,1,32]{1,3,2,0:T(8,128)S(1)}, u32[]{:S(2)}, u32[]{:S(2)}) collective-permute-start(f32[2,8,1,32]{1,3,2,0:T(8,128)S(1)} %get-tuple-element.26), channel_id=1, source_target_pairs={{4,0},{8,4},{12,8},{16,12},{20,16},{24,20},{28,24},{5,1},{9,5},{13... | collective-permute-start | bytes 6152 | tf_op jit(solution)/shard_map/ppermute | solution.py:22
  97.8 17.3 %collective-permute-start.40 = (f32[2,8,1,32]{1,3,2,0:T(8,128)S(1)}, f32[2,8,1,32]{1,3,2,0:T(8,128)S(1)}, u32[]{:S(2)}, u32[]{:S(2)}) collective-permute-start(f32[2,8,1,32]{1,3,2,0:T(8,128)S(1)} %get-tuple-element.25), channel_id=1, source_target_pairs={{0,4},{4,8},{8,12},{12,16},{16,20},{20,24},{24,28},{1,5},{5,9},{9,... | collective-permute-start | bytes 6152 | tf_op jit(solution)/shard_map/ppermute | solution.py:19
  106.6 18.7 %collective-permute-start.23 = (f32[2,8,16,1]{3,2,1,0:T(8,128)S(1)}, f32[2,8,16,1]{3,2,1,0:T(8,128)S(1)}, u32[]{:S(2)}, u32[]{:S(2)}) collective-permute-start(f32[2,8,16,1]{3,2,1,0:T(8,128)S(1)} %get-tuple-element.48), channel_id=1, source_target_pairs={{1,0},{2,1},{3,2},{0,3},{5,4},{6,5},{7,6},{4,7},{9,8},{10,9},{11,1... | collective-permute-start | bytes 3080 | tf_op jit(solution)/shard_map/ppermute | solution.py:22
  115.1 22.3 %collective-permute-start.20 = (f32[2,8,1,64]{3,2,1,0:T(1,128)S(1)}, f32[2,8,1,64]{3,2,1,0:T(1,128)S(1)}, u32[]{:S(2)}, u32[]{:S(2)}) collective-permute-start(f32[2,8,1,64]{3,2,1,0:T(1,128)S(1)} %get-tuple-element.45), channel_id=1, source_target_pairs={{0,4},{4,8},{8,12},{12,16},{16,20},{20,24},{24,28},{1,5},{5,9},{9,... | collective-permute-start | bytes 12296 | tf_op jit(solution)/shard_map/ppermute | solution.py:19
  125.3 33.0 %collective-permute-start.2 = (f32[2,8,32,1]{2,1,3,0:T(8,128)}, f32[2,8,32,1]{2,1,3,0:T(8,128)S(1)}, u32[]{:S(2)}, u32[]{:S(2)}) collective-permute-start(f32[2,8,32,1]{2,1,3,0:T(8,128)} %get-tuple-element.19), channel_id=1, source_target_pairs={{0,1},{1,2},{2,3},{3,0},{4,5},{5,6},{6,7},{7,4},{8,9},{9,10},{10,1... | collective-permute-start | bytes 6152 | tf_op jit(solution)/shard_map/ppermute | solution.py:19
  128.6 18.3 %collective-permute-start = (f32[2,8,1,128]{3,1,2,0:T(8,128)S(1)}, f32[2,8,1,128]{3,1,2,0:T(8,128)S(1)}, u32[]{:S(2)}, u32[]{:S(2)}) collective-permute-start(f32[2,8,1,128]{3,1,2,0:T(8,128)S(1)} %copy.348), channel_id=1, source_target_pairs={{0,4},{4,8},{8,12},{12,16},{16,20},{20,24},{24,28},{1,5},{5,9},{9,... | collective-permute-start | bytes 24584 | tf_op jit(solution)/shard_map/ppermute | solution.py:19
  137.4 32.2 %collective-permute-start.47 = (f32[2,8,8,1]{1,3,2,0:T(1,128)}, f32[2,8,8,1]{1,3,2,0:T(1,128)}, u32[]{:S(2)}, u32[]{:S(2)}) collective-permute-start(f32[2,8,8,1]{1,3,2,0:T(1,128)} %get-tuple-element.24), channel_id=1, source_target_pairs={{1,0},{2,1},{3,2},{0,3},{5,4},{6,5},{7,6},{4,7},{9,8},{10,9},{11,1... | collective-permute-start | bytes 1544 | tf_op jit(solution)/shard_map/ppermute | solution.py:22
  143.5 28.0 %collective-permute-start.46 = (f32[2,8,8,1]{1,3,2,0:T(1,128)}, f32[2,8,8,1]{1,3,2,0:T(1,128)}, u32[]{:S(2)}, u32[]{:S(2)}) collective-permute-start(f32[2,8,8,1]{1,3,2,0:T(1,128)} %get-tuple-element.23), channel_id=1, source_target_pairs={{0,1},{1,2},{2,3},{3,0},{4,5},{5,6},{6,7},{7,4},{8,9},{9,10},{10,1... | collective-permute-start | bytes 1544 | tf_op jit(solution)/shard_map/ppermute | solution.py:19
  146.8 26.0 %collective-permute-start.45 = (f32[2,8,1,32]{1,3,2,0:T(8,128)}, f32[2,8,1,32]{1,3,2,0:T(8,128)}, u32[]{:S(2)}, u32[]{:S(2)}) collective-permute-start(f32[2,8,1,32]{1,3,2,0:T(8,128)} %get-tuple-element.22), channel_id=1, source_target_pairs={{4,0},{8,4},{12,8},{16,12},{20,16},{24,20},{28,24},{5,1},{9,5},{13... | collective-permute-start | bytes 6152 | tf_op jit(solution)/shard_map/ppermute | solution.py:22
  149.5 32.7 %collective-permute-start.44 = (f32[2,8,1,32]{1,3,2,0:T(8,128)}, f32[2,8,1,32]{1,3,2,0:T(8,128)S(1)}, u32[]{:S(2)}, u32[]{:S(2)}) collective-permute-start(f32[2,8,1,32]{1,3,2,0:T(8,128)} %get-tuple-element.21), channel_id=1, source_target_pairs={{0,4},{4,8},{8,12},{12,16},{16,20},{20,24},{24,28},{1,5},{5,9},{9,... | collective-permute-start | bytes 6152 | tf_op jit(solution)/shard_map/ppermute | solution.py:19
  158.9 37.2 %collective-permute-start.27 = (f32[2,8,16,1]{3,2,1,0:T(8,128)}, f32[2,8,16,1]{3,2,1,0:T(8,128)}, u32[]{:S(2)}, u32[]{:S(2)}) collective-permute-start(f32[2,8,16,1]{3,2,1,0:T(8,128)} %get-tuple-element.44), channel_id=1, source_target_pairs={{1,0},{2,1},{3,2},{0,3},{5,4},{6,5},{7,6},{4,7},{9,8},{10,9},{11,1... | collective-permute-start | bytes 3080 | tf_op jit(solution)/shard_map/ppermute | solution.py:22
  169.6 28.4 %collective-permute-start.26 = (f32[2,8,16,1]{3,2,1,0:T(8,128)}, f32[2,8,16,1]{3,2,1,0:T(8,128)}, u32[]{:S(2)}, u32[]{:S(2)}) collective-permute-start(f32[2,8,16,1]{3,2,1,0:T(8,128)} %get-tuple-element.43), channel_id=1, source_target_pairs={{0,1},{1,2},{2,3},{3,0},{4,5},{5,6},{6,7},{7,4},{8,9},{9,10},{10,1... | collective-permute-start | bytes 3080 | tf_op jit(solution)/shard_map/ppermute | solution.py:19
  171.5 27.8 %collective-permute-start.25 = (f32[2,8,1,64]{3,2,1,0:T(1,128)}, f32[2,8,1,64]{3,2,1,0:T(1,128)S(1)}, u32[]{:S(2)}, u32[]{:S(2)}) collective-permute-start(f32[2,8,1,64]{3,2,1,0:T(1,128)} %get-tuple-element.42), channel_id=1, source_target_pairs={{4,0},{8,4},{12,8},{16,12},{20,16},{24,20},{28,24},{5,1},{9,5},{13... | collective-permute-start | bytes 12296 | tf_op jit(solution)/shard_map/ppermute | solution.py:22
  172.8 34.8 %collective-permute-start.24 = (f32[2,8,1,64]{3,2,1,0:T(1,128)}, f32[2,8,1,64]{3,2,1,0:T(1,128)}, u32[]{:S(2)}, u32[]{:S(2)}) collective-permute-start(f32[2,8,1,64]{3,2,1,0:T(1,128)} %get-tuple-element.41), channel_id=1, source_target_pairs={{0,4},{4,8},{8,12},{12,16},{16,20},{20,24},{24,28},{1,5},{5,9},{9,... | collective-permute-start | bytes 12296 | tf_op jit(solution)/shard_map/ppermute | solution.py:19
  187.8 24.6 %collective-permute-start.7 = (f32[2,8,32,1]{2,1,3,0:T(8,128)}, f32[2,8,32,1]{2,1,3,0:T(8,128)S(1)}, u32[]{:S(2)}, u32[]{:S(2)}) collective-permute-start(f32[2,8,32,1]{2,1,3,0:T(8,128)} %get-tuple-element.16), channel_id=1, source_target_pairs={{1,0},{2,1},{3,2},{0,3},{5,4},{6,5},{7,6},{4,7},{9,8},{10,9},{11,1... | collective-permute-start | bytes 6152 | tf_op jit(solution)/shard_map/ppermute | solution.py:22
  216.8 32.0 %collective-permute-start.11 = (f32[2,8,32,1]{2,1,3,0:T(8,128)}, f32[2,8,32,1]{2,1,3,0:T(8,128)S(1)}, u32[]{:S(2)}, u32[]{:S(2)}) collective-permute-start(f32[2,8,32,1]{2,1,3,0:T(8,128)} %get-tuple-element.12), channel_id=1, source_target_pairs={{1,0},{2,1},{3,2},{0,3},{5,4},{6,5},{7,6},{4,7},{9,8},{10,9},{11,1... | collective-permute-start | bytes 6152 | tf_op jit(solution)/shard_map/ppermute | solution.py:22
  222.0 36.3 %collective-permute-start.10 = (f32[2,8,32,1]{2,1,3,0:T(8,128)}, f32[2,8,32,1]{2,1,3,0:T(8,128)}, u32[]{:S(2)}, u32[]{:S(2)}) collective-permute-start(f32[2,8,32,1]{2,1,3,0:T(8,128)} %get-tuple-element.11), channel_id=1, source_target_pairs={{0,1},{1,2},{2,3},{3,0},{4,5},{5,6},{6,7},{7,4},{8,9},{9,10},{10,1... | collective-permute-start | bytes 6152 | tf_op jit(solution)/shard_map/ppermute | solution.py:19
  228.3 17.9 %collective-permute-start.8 = (f32[2,8,1,128]{3,1,2,0:T(8,128)}, f32[2,8,1,128]{3,1,2,0:T(8,128)S(1)}, u32[]{:S(2)}, u32[]{:S(2)}) collective-permute-start(f32[2,8,1,128]{3,1,2,0:T(8,128)} %copy.356), channel_id=1, source_target_pairs={{0,4},{4,8},{8,12},{12,16},{16,20},{20,24},{24,28},{1,5},{5,9},{9,... | collective-permute-start | bytes 24584 | tf_op jit(solution)/shard_map/ppermute | solution.py:19
  237.7 33.2 %collective-permute-start.31 = (f32[2,8,16,1]{3,2,1,0:T(8,128)}, f32[2,8,16,1]{3,2,1,0:T(8,128)}, u32[]{:S(2)}, u32[]{:S(2)}) collective-permute-start(f32[2,8,16,1]{3,2,1,0:T(8,128)} %get-tuple-element.40), channel_id=1, source_target_pairs={{1,0},{2,1},{3,2},{0,3},{5,4},{6,5},{7,6},{4,7},{9,8},{10,9},{11,1... | collective-permute-start | bytes 3080 | tf_op jit(solution)/shard_map/ppermute | solution.py:22
  242.9 30.0 %collective-permute-start.30 = (f32[2,8,16,1]{3,2,1,0:T(8,128)S(1)}, f32[2,8,16,1]{3,2,1,0:T(8,128)}, u32[]{:S(2)}, u32[]{:S(2)}) collective-permute-start(f32[2,8,16,1]{3,2,1,0:T(8,128)S(1)} %get-tuple-element.39), channel_id=1, source_target_pairs={{0,1},{1,2},{2,3},{3,0},{4,5},{5,6},{6,7},{7,4},{8,9},{9,10},{10,1... | collective-permute-start | bytes 3080 | tf_op jit(solution)/shard_map/ppermute | solution.py:19
  246.2 27.9 %collective-permute-start.29 = (f32[2,8,1,64]{3,2,1,0:T(1,128)}, f32[2,8,1,64]{3,2,1,0:T(1,128)S(1)}, u32[]{:S(2)}, u32[]{:S(2)}) collective-permute-start(f32[2,8,1,64]{3,2,1,0:T(1,128)} %get-tuple-element.38), channel_id=1, source_target_pairs={{4,0},{8,4},{12,8},{16,12},{20,16},{24,20},{28,24},{5,1},{9,5},{13... | collective-permute-start | bytes 12296 | tf_op jit(solution)/shard_map/ppermute | solution.py:22
  248.9 34.1 %collective-permute-start.28 = (f32[2,8,1,64]{3,2,1,0:T(1,128)}, f32[2,8,1,64]{3,2,1,0:T(1,128)}, u32[]{:S(2)}, u32[]{:S(2)}) collective-permute-start(f32[2,8,1,64]{3,2,1,0:T(1,128)} %get-tuple-element.37), channel_id=1, source_target_pairs={{0,4},{4,8},{8,12},{12,16},{16,20},{20,24},{24,28},{1,5},{5,9},{9,... | collective-permute-start | bytes 12296 | tf_op jit(solution)/shard_map/ppermute | solution.py:19
  262.7 25.8 %collective-permute-start.15 = (f32[2,8,32,1]{2,1,3,0:T(8,128)}, f32[2,8,32,1]{2,1,3,0:T(8,128)S(1)}, u32[]{:S(2)}, u32[]{:S(2)}) collective-permute-start(f32[2,8,32,1]{2,1,3,0:T(8,128)} %get-tuple-element.8), channel_id=1, source_target_pairs={{1,0},{2,1},{3,2},{0,3},{5,4},{6,5},{7,6},{4,7},{9,8},{10,9},{11,1... | collective-permute-start | bytes 6152 | tf_op jit(solution)/shard_map/ppermute | solution.py:22
  270.9 17.5 %collective-permute-start.14 = (f32[2,8,32,1]{2,1,3,0:T(8,128)}, f32[2,8,32,1]{2,1,3,0:T(8,128)}, u32[]{:S(2)}, u32[]{:S(2)}) collective-permute-start(f32[2,8,32,1]{2,1,3,0:T(8,128)} %get-tuple-element.7), channel_id=1, source_target_pairs={{0,1},{1,2},{2,3},{3,0},{4,5},{5,6},{6,7},{7,4},{8,9},{9,10},{10,1... | collective-permute-start | bytes 6152 | tf_op jit(solution)/shard_map/ppermute | solution.py:19
  (25 other events, 343.9 us)
Sparse Core Ops, SparseCore 0:
  294.8 58.9 all-gather.2
